TPU v7x, 32 devices: a whole 2x2x4 slice. The times are simulated.
32 devices in a mesh: gx: 4 (over z), gy: 8 (over y, x, core).
Axes of the slice: x: 2, y: 2, z: 4, core: 2. Of those that a mesh axis runs over, the one named last changes fastest.
Arguments:
- right_side: float32 [512, 2048], P('gx', 'gy'), may hold values from -1.2 to 1.2
- shift: float32 [512, 2048], P('gx', 'gy'), may hold values from 0.0001 to 0.004
Outputs:
- solution: float32 [512, 2048], P('gx', 'gy')
- residual: float32 [512, 2048], P('gx', 'gy')
All inputs are finite; a program needn't handle non-finite values.
Results may differ from a plain program's by a relative error of at most 0.0003.
Values sent between devices are 32-bit elements; how exact they have to be, the bound alone decides.
A program may use at most 128 MiB of HBM per device.

v0:
```python
import jax
import jax.numpy as jnp
from jax import lax
from jax.sharding import PartitionSpec as P

LEVELS = 4
COARSE_SWEEPS = 6
damping = 0.8


def padded_2(cells, sides, width):
    for axis, dim in sides:
        count = lax.axis_size(axis)
        ends = count - 1
        head = lax.slice_in_dim(cells, 0, width, axis=dim)
        tail = lax.slice_in_dim(cells, cells.shape[dim] - width, cells.shape[dim], axis=dim)
        cells = jnp.concatenate(
            [
                lax.ppermute(tail, axis, [(i, (i + 1) % count) for i in range(ends)]),
                cells,
                lax.ppermute(head, axis, [((i + 1) % count, i) for i in range(ends)]),
            ],
            axis=dim,
        )
    return cells


def restrict(values):
    rows, columns = values.shape
    blocks = values.reshape(rows // 2, 2, columns // 2, 2)
    return 0.25 * (
        blocks[:, 0, :, 0] + blocks[:, 1, :, 0] + blocks[:, 0, :, 1] + blocks[:, 1, :, 1]
    )


def prolong(values):
    rows, columns = values.shape
    copies = jnp.broadcast_to(values[:, None, :, None], (rows, 2, columns, 2))
    return copies.reshape(2 * rows, 2 * columns)


def operate_padded(padded, shifts, level):
    centre = padded[1:-1, 1:-1]
    beside = padded[2:, 1:-1] + padded[:-2, 1:-1] + padded[1:-1, 2:] + padded[1:-1, :-2]
    return 4.0 ** (-level) * (4.0 * centre - beside) + shifts * centre


def with_rim(field):
    return padded_2(field, (("gx", 0), ("gy", 1)), 1)


def build_levels(shift):
    levels = []
    shifts = shift
    for level in range(LEVELS + 1):
        diagonal = 4.0 ** (1 - level) + shifts
        outer_shift = None
        inside = None
        levels.append((shifts, diagonal, outer_shift, inside))
        if level < LEVELS:
            shifts = restrict(shifts)
    return levels


def sweep_once(iterate, source, section, level):
    shifts, diagonal = (section[0], section[1])
    if iterate is None:
        return damping * source / diagonal
    return (
        iterate + damping * (source - operate_padded(with_rim(iterate), shifts, level)) / diagonal
    )


def smooth_two(iterate, source, section, level):
    iterate = sweep_once(iterate, source, section, level)
    return sweep_once(iterate, source, section, level)


def residual_of(iterate, source, section, level):
    return source - operate_padded(with_rim(iterate), section[0], level)


def gather_early(field):
    row_band = lax.all_gather(field, "gy", axis=1, tiled=True)
    return lax.all_gather(row_band, "gx", axis=0, tiled=True)


def local_sweeps(iterate, source, shifts, level, count):
    diagonal = 4.0 ** (1 - level) + shifts
    for turn in range(count):
        if iterate is None:
            iterate = damping * source / diagonal
        else:
            iterate = (
                iterate
                + damping * (source - operate_padded(jnp.pad(iterate, 1), shifts, level)) / diagonal
            )
    return iterate


def local_coarse(iterate, source, shifts):
    unit_total = jnp.sum(operate_padded(jnp.pad(jnp.ones_like(source), 1), shifts, LEVELS))
    if iterate is None:
        left = jnp.sum(source)
        iterate = jnp.zeros_like(source) + left / unit_total
    else:
        left = jnp.sum(source - operate_padded(jnp.pad(iterate, 1), shifts, LEVELS))
        iterate = iterate + left / unit_total
    return local_sweeps(iterate, source, shifts, LEVELS, COARSE_SWEEPS)


def local_vcycle(level, iterate, source, shift_table):
    shifts = shift_table[level]
    if level == LEVELS:
        return local_coarse(iterate, source, shifts)
    iterate = local_sweeps(iterate, source, shifts, level, 2)
    coarse_rhs = restrict(source - operate_padded(jnp.pad(iterate, 1), shifts, level))
    iterate = iterate + prolong(local_vcycle(level + 1, None, coarse_rhs, shift_table))
    return local_sweeps(iterate, source, shifts, level, 2)


def local_fcycle(level, source, shift_table):
    shifts = shift_table[level]
    if level == LEVELS:
        return local_coarse(None, source, shifts)
    iterate = local_sweeps(None, source, shifts, level, 2)
    coarse_rhs = restrict(source - operate_padded(jnp.pad(iterate, 1), shifts, level))
    correction = local_fcycle(level + 1, coarse_rhs, shift_table)
    correction = local_vcycle(level + 1, correction, coarse_rhs, shift_table)
    iterate = iterate + prolong(correction)
    return local_sweeps(iterate, source, shifts, level, 2)


def own_block(whole, rows, columns):
    return lax.dynamic_slice(
        whole, (lax.axis_index("gx") * rows, lax.axis_index("gy") * columns), (rows, columns)
    )


def early_solve(coarse_rhs, shift_table, full):
    whole_rhs = gather_early(coarse_rhs)
    if full:
        whole = local_fcycle(LEVELS - 1, whole_rhs, shift_table)
        whole = local_vcycle(LEVELS - 1, whole, whole_rhs, shift_table)
    else:
        whole = local_vcycle(LEVELS - 1, None, whole_rhs, shift_table)
    return own_block(whole, coarse_rhs.shape[0], coarse_rhs.shape[1])


def vcycle(level, iterate, source, levels, shift_whole):
    section = levels[level]
    iterate = smooth_two(iterate, source, section, level)
    coarse_rhs = restrict(residual_of(iterate, source, section, level))
    if level + 1 == LEVELS - 1:
        correction = early_solve(coarse_rhs, shift_whole, False)
    else:
        correction = vcycle(level + 1, None, coarse_rhs, levels, shift_whole)
    iterate = iterate + prolong(correction)
    return smooth_two(iterate, source, section, level)


def fcycle(level, source, levels, shift_whole):
    section = levels[level]
    iterate = smooth_two(None, source, section, level)
    coarse_rhs = restrict(residual_of(iterate, source, section, level))
    if level + 1 == LEVELS - 1:
        correction = early_solve(coarse_rhs, shift_whole, True)
    else:
        correction = fcycle(level + 1, coarse_rhs, levels, shift_whole)
        correction = vcycle(level + 1, correction, coarse_rhs, levels, shift_whole)
    iterate = iterate + prolong(correction)
    return smooth_two(iterate, source, section, level)


def body(right_side, shift):
    levels = build_levels(shift)
    upper = gather_early(levels[LEVELS - 1][0])
    shift_whole = {LEVELS - 1: upper, LEVELS: restrict(upper)}
    solution = fcycle(0, right_side, levels, shift_whole)
    residual = residual_of(solution, right_side, levels[0], 0)
    return (solution, residual)


def solution(mesh):
    in_specs = (P("gx", "gy"), P("gx", "gy"))
    out_specs = (P("gx", "gy"), P("gx", "gy"))
    return jax.shard_map(body, mesh=mesh, in_specs=in_specs, out_specs=out_specs, check_vma=False)
```

profile of v0, /device:TPU:28, one launch (start us, length us, event | category | flops | bytes accessed | tf_op | source)
XLA Modules:
  0.0 715.0 jit_solution(5198619085677997498)
XLA Ops:
  5.3 10.5 %reshape.185 = f32[64,2,128,2]{3,2,1,0:T(8,128)} reshape(f32[128,256]{1,0:T(8,128)} %param.3) | data formatting | bytes 262144 | tf_op jit(solution)/shard_map/reshape | solution.py:30
  20.4 8.0 %fusion.1 = f32[64,128]{1,0:T(8,128)S(1)} fusion(f32[64,2,128,2]{3,2,1,0:T(8,128)} %reshape.185), kind=kLoop, calls=%fused_computation.2 | loop fusion | flops 32768 | bytes 163840 | tf_op jit(solution)/shard_map/mul | solution.py:31
  50.5 9.8 %reshape.184 = f32[64,2,128,2]{3,2,1,0:T(8,128)} reshape(f32[128,256]{1,0:T(8,128)S(1)} %fusion.39) | data formatting | bytes 262144 | tf_op jit(solution)/shard_map/reshape | solution.py:30
  60.3 8.5 %multiply_reduce_fusion = (f32[64,128]{1,0:T(8,128)S(1)}, f32[64,128]{1,0:T(8,128)S(1)}) fusion(f32[64,2,128,2]{3,2,1,0:T(8,128)} %reshape.184), kind=kLoop, calls=%fused_computation.8 | loop fusion | flops 40960 | bytes 196608 | tf_op jit(solution)/shard_map/mul | solution.py:31
  72.8 14.8 %all-gather.2 = f32[16,1,256,1]{3,2,1,0:T(8,128)S(1)} all-gather(f32[16,1,32,1]{3,2,1,0:T(8,128)S(1)} %fusion.10), channel_id=4, replica_groups=mesh['gx'=4,'gy'=8] {'gy'}, dimensions={2}, use_global_device_ids=true | all-gather | bytes 18432 | tf_op jit(solution)/shard_map/all_gather | solution.py:84
  93.7 13.6 %all-gather.3 = f32[64,1,256,1]{2,3,1,0:T(1,128)S(1)} all-gather(f32[16,1,256,1]{2,3,1,0:T(1,128)S(1)} %copy.135), channel_id=5, replica_groups=mesh['gx'=4,'gy'=8] {'gx'}, dimensions={0}, use_global_device_ids=true | all-gather | bytes 81920 | tf_op jit(solution)/shard_map/all_gather | solution.py:85
  111.4 5.6 reshape.189
  128.6 4.5 collective-permute-start.16
  163.9 14.8 %all-gather = f32[16,1,256,1]{3,2,1,0:T(8,128)S(1)} all-gather(f32[16,1,32,1]{3,2,1,0:T(8,128)S(1)} %fusion.11), channel_id=2, replica_groups=mesh['gx'=4,'gy'=8] {'gy'}, dimensions={2}, use_global_device_ids=true | all-gather | bytes 18432 | tf_op jit(solution)/shard_map/all_gather | solution.py:84
  179.3 13.1 %all-gather.1 = f32[64,1,256,1]{2,3,1,0:T(1,128)S(1)} all-gather(f32[16,1,256,1]{2,3,1,0:T(1,128)S(1)} %copy.134), channel_id=3, replica_groups=mesh['gx'=4,'gy'=8] {'gx'}, dimensions={0}, use_global_device_ids=true | all-gather | bytes 81920 | tf_op jit(solution)/shard_map/all_gather | solution.py:85
  192.7 5.6 reshape.188
  198.3 8.6 %multiply_reduce_fusion.6 = (f32[32,128]{1,0:T(8,128)S(1)}, f32[32,1,128,1]{3,2,1,0:T(8,128)S(1)}, f32[]{:T(128)}, f32[32,128]{1,0:T(8,128)S(1)}) fusion(f32[32,2,128,2]{3,2,1,0:T(8,128)} %reshape.189, f32[32,2,128,2]{3,2,1,0:T(8,128)} %reshape.188), kind=kLoop, calls=%fused_computation.33 | loop fusion | flops 36863 | bytes 180228 | tf_op jit(solution)/shard_map/mul | solution.py:31
  220.0 5.6 reshape.191
  225.6 5.8 fusion.727
  241.3 10.9 %collective-permute-start.24 = (f32[1,64]{1,0:T(1,128)S(1)}, f32[1,64]{1,0:T(1,128)S(1)}, u32[]{:S(2)}, u32[]{:S(2)}) collective-permute-start(f32[1,64]{1,0:T(1,128)S(1)} %get-tuple-element.123), channel_id=1, source_target_pairs={{8,0},{16,8},{24,16},{9,1},{17,9},{25,17},{10,2},{18,10},{26,18},{... | collective-permute-start | bytes 776 | tf_op jit(solution)/shard_map/ppermute | solution.py:21
  331.4 15.1 %all-gather.4 = f32[16,1,256,1]{3,2,1,0:T(8,128)} all-gather(f32[16,1,32,1]{3,2,1,0:T(8,128)S(1)} %fusion.9), channel_id=6, replica_groups=mesh['gx'=4,'gy'=8] {'gy'}, dimensions={2}, use_global_device_ids=true | all-gather | bytes 18432 | tf_op jit(solution)/shard_map/all_gather | solution.py:84
  348.7 13.1 %all-gather.5 = f32[64,1,256,1]{2,3,1,0:T(1,128)S(1)} all-gather(f32[16,1,256,1]{2,3,1,0:T(1,128)S(1)} %copy.136), channel_id=7, replica_groups=mesh['gx'=4,'gy'=8] {'gx'}, dimensions={0}, use_global_device_ids=true | all-gather | bytes 81920 | tf_op jit(solution)/shard_map/all_gather | solution.py:85
  362.1 5.6 reshape.195
  367.7 5.8 fusion.726
  537.2 15.1 %all-gather.6 = f32[16,1,256,1]{3,2,1,0:T(8,128)} all-gather(f32[16,1,32,1]{3,2,1,0:T(8,128)S(1)} %fusion.8), channel_id=8, replica_groups=mesh['gx'=4,'gy'=8] {'gy'}, dimensions={2}, use_global_device_ids=true | all-gather | bytes 18432 | tf_op jit(solution)/shard_map/all_gather | solution.py:84
  554.5 13.1 %all-gather.7 = f32[64,1,256,1]{2,3,1,0:T(1,128)S(1)} all-gather(f32[16,1,256,1]{2,3,1,0:T(1,128)S(1)} %copy.137), channel_id=9, replica_groups=mesh['gx'=4,'gy'=8] {'gx'}, dimensions={0}, use_global_device_ids=true | all-gather | bytes 81920 | tf_op jit(solution)/shard_map/all_gather | solution.py:85
  567.9 5.6 reshape.201
  573.4 5.8 fusion.725
  658.5 6.9 reshape.205
  (449 shorter events, 478.9 us)
Async XLA Ops:
  1.6 14.2 %collective-permute-start = (f32[1,256]{1,0:T(1,128)S(1)}, f32[1,256]{1,0:T(1,128)S(1)}, u32[]{:S(2)}, u32[]{:S(2)}) collective-permute-start(f32[1,256]{1,0:T(1,128)S(1)} %get-tuple-element.37), channel_id=1, source_target_pairs={{8,0},{16,8},{24,16},{9,1},{17,9},{25,17},{10,2},{18,10},{26,18},{... | collective-permute-start | bytes 3080 | tf_op jit(solution)/shard_map/ppermute | solution.py:21
  4.0 11.8 %collective-permute-start.1 = (f32[1,256]{1,0:T(1,128)S(1)}, f32[1,256]{1,0:T(1,128)S(1)}, u32[]{:S(2)}, u32[]{:S(2)}) collective-permute-start(f32[1,256]{1,0:T(1,128)S(1)} %get-tuple-element.36), channel_id=1, source_target_pairs={{0,8},{8,16},{16,24},{1,9},{9,17},{17,25},{2,10},{10,18},{18,26},{... | collective-permute-start | bytes 3080 | tf_op jit(solution)/shard_map/ppermute | solution.py:19
  16.0 14.6 %collective-permute-start.2 = (f32[130,1]{1,0:T(8,128)S(1)}, f32[130,1]{1,0:T(8,128)S(1)}, u32[]{:S(2)}, u32[]{:S(2)}) collective-permute-start(f32[130,1]{1,0:T(8,128)S(1)} %get-tuple-element.26), channel_id=1, source_target_pairs={{1,0},{2,1},{3,2},{4,3},{5,4},{6,5},{7,6},{9,8},{10,9},{11,10},{12... | collective-permute-start | bytes 1568 | tf_op jit(solution)/shard_map/ppermute | solution.py:21
  18.5 12.1 %collective-permute-start.3 = (f32[130,1]{1,0:T(8,128)S(1)}, f32[130,1]{1,0:T(8,128)S(1)}, u32[]{:S(2)}, u32[]{:S(2)}) collective-permute-start(f32[130,1]{1,0:T(8,128)S(1)} %get-tuple-element.27), channel_id=1, source_target_pairs={{0,1},{1,2},{2,3},{3,4},{4,5},{5,6},{6,7},{8,9},{9,10},{10,11},{11... | collective-permute-start | bytes 1568 | tf_op jit(solution)/shard_map/ppermute | solution.py:19
  30.7 7.2 %collective-permute-start.4 = (f32[1,256]{1,0:T(1,128)S(1)}, f32[1,256]{1,0:T(1,128)S(1)}, u32[]{:S(2)}, u32[]{:S(2)}) collective-permute-start(f32[1,256]{1,0:T(1,128)S(1)} %get-tuple-element.35), channel_id=1, source_target_pairs={{8,0},{16,8},{24,16},{9,1},{17,9},{25,17},{10,2},{18,10},{26,18},{... | collective-permute-start | bytes 3080 | tf_op jit(solution)/shard_map/ppermute | solution.py:21
  43.8 6.5 collective-permute-start.7
  68.9 19.4 %collective-permute-start.8 = (f32[1,128]{1,0:T(1,128)S(1)}, f32[1,128]{1,0:T(1,128)S(1)}, u32[]{:S(2)}, u32[]{:S(2)}) collective-permute-start(f32[1,128]{1,0:T(1,128)S(1)} %get-tuple-element.75), channel_id=1, source_target_pairs={{8,0},{16,8},{24,16},{9,1},{17,9},{25,17},{10,2},{18,10},{26,18},{... | collective-permute-start | bytes 1544 | tf_op jit(solution)/shard_map/ppermute | solution.py:21
  71.5 16.8 %collective-permute-start.9 = (f32[1,128]{1,0:T(1,128)S(1)}, f32[1,128]{1,0:T(1,128)S(1)}, u32[]{:S(2)}, u32[]{:S(2)}) collective-permute-start(f32[1,128]{1,0:T(1,128)S(1)} %get-tuple-element.74), channel_id=1, source_target_pairs={{0,8},{8,16},{16,24},{1,9},{9,17},{17,25},{2,10},{10,18},{18,26},{... | collective-permute-start | bytes 1544 | tf_op jit(solution)/shard_map/ppermute | solution.py:19
  88.4 18.9 %collective-permute-start.10 = (f32[66,1]{1,0:T(8,128)S(1)}, f32[66,1]{1,0:T(8,128)S(1)}, u32[]{:S(2)}, u32[]{:S(2)}) collective-permute-start(f32[66,1]{1,0:T(8,128)S(1)} %get-tuple-element.56), channel_id=1, source_target_pairs={{1,0},{2,1},{3,2},{4,3},{5,4},{6,5},{7,6},{9,8},{10,9},{11,10},{12... | collective-permute-start | bytes 800 | tf_op jit(solution)/shard_map/ppermute | solution.py:21
  91.7 15.5 %collective-permute-start.11 = (f32[66,1]{1,0:T(8,128)S(1)}, f32[66,1]{1,0:T(8,128)S(1)}, u32[]{:S(2)}, u32[]{:S(2)}) collective-permute-start(f32[66,1]{1,0:T(8,128)S(1)} %get-tuple-element.57), channel_id=1, source_target_pairs={{0,1},{1,2},{2,3},{3,4},{4,5},{5,6},{6,7},{8,9},{9,10},{10,11},{11... | collective-permute-start | bytes 800 | tf_op jit(solution)/shard_map/ppermute | solution.py:19
  107.4 9.6 %collective-permute-start.12 = (f32[1,128]{1,0:T(1,128)S(1)}, f32[1,128]{1,0:T(1,128)S(1)}, u32[]{:S(2)}, u32[]{:S(2)}) collective-permute-start(f32[1,128]{1,0:T(1,128)S(1)} %get-tuple-element.73), channel_id=1, source_target_pairs={{8,0},{16,8},{24,16},{9,1},{17,9},{25,17},{10,2},{18,10},{26,18},{... | collective-permute-start | bytes 1544 | tf_op jit(solution)/shard_map/ppermute | solution.py:21
  110.0 7.0 collective-permute-start.13
  119.0 6.2 collective-permute-start.15
  241.3 12.2 %collective-permute-start.24 = (f32[1,64]{1,0:T(1,128)S(1)}, f32[1,64]{1,0:T(1,128)S(1)}, u32[]{:S(2)}, u32[]{:S(2)}) collective-permute-start(f32[1,64]{1,0:T(1,128)S(1)} %get-tuple-element.123), channel_id=1, source_target_pairs={{8,0},{16,8},{24,16},{9,1},{17,9},{25,17},{10,2},{18,10},{26,18},{... | collective-permute-start | bytes 776 | tf_op jit(solution)/shard_map/ppermute | solution.py:21
  429.3 6.2 collective-permute-start.55
  445.0 6.2 collective-permute-start.59
  460.9 6.2 collective-permute-start.63
  476.7 6.2 collective-permute-start.67
  492.4 6.2 collective-permute-start.71
  632.5 6.2 collective-permute-start.91
  648.2 6.2 collective-permute-start.95
  674.9 6.5 collective-permute-start.99
  691.0 6.5 collective-permute-start.103
  707.2 6.5 collective-permute-start.107
  (87 other events, 419.7 us)
where the time goes:
time: 727 us; the launch traced here: 715 us
  starting transfers between devices  227 us (31%)
  waiting for transfers between devices  192 us (26%)
  blocking collectives  113 us (16%)
  local copies, waits for them, and re-layouts  110 us (15%)
  other arithmetic  62.6 us (9%)
  between operations  10.1 us (1%)
    ppermute x54, waiting for transfers between devices, padded_2(): lax.ppermute(tail, axis, [(i, (i + 1) % count) for i in range(ends)])  191 us
    ppermute x54, starting transfers between devices, padded_2(): lax.ppermute(head, axis, [((i + 1) % count, i) for i in range(ends)])  129 us
    ppermute x54, starting transfers between devices, padded_2(): lax.ppermute(tail, axis, [(i, (i + 1) % count) for i in range(ends)])  98.4 us
    all_gather x4, blocking collectives, gather_early(): row_band = lax.all_gather(field, 'gy', axis=1, tiled=True)  59.9 us
    reshape x12, local copies, waits for them, and re-layouts, restrict(): blocks = values.reshape(rows // 2, 2, columns // 2, 2)  55.2 us
    all_gather x4, blocking collectives, gather_early(): return lax.all_gather(row_band, 'gx', axis=0, tiled=True)  53 us
    mul x13, other arithmetic, restrict(): 0.25 * (blocks[:, 0, :, 0] + blocks[:, 1, :, 0] + blocks[:, 0, :, 1] + bl...  48.9 us
    reshape x10, local copies, waits for them, and re-layouts, prolong(): return copies.reshape(2 * rows, 2 * columns)  27.8 us
  transfers between devices with their start and end apart: 108, of which 49 were waited for; matrix products, arithmetic and copies ran while one was open for 4% of the time, Pallas kernels for 0%

commit v1 on v0

--- a/solution.py
+++ b/solution.py
@@ -81,7 +81,8 @@
 
 
 def gather_early(field):
-    row_band = lax.all_gather(field, "gy", axis=1, tiled=True)
+    pieces = lax.all_gather(field, "gy")
+    row_band = jnp.concatenate(pieces, axis=1)
     return lax.all_gather(row_band, "gx", axis=0, tiled=True)
 
 

time: 727 us -> 697 us (0.959)
  blocking collectives: 113 us -> 84.9 us
  starting transfers between devices: 227 us -> 216 us
    all_gather x4, blocking collectives: 59.9 us -> 32.2 us  [gather_early(): pieces = lax.all_gather(field, 'gy')]
    ppermute x54, starting transfers between devices: 129 us -> 116 us  [padded_2(): lax.ppermute(head, axis, [((i + 1) % count, i) for i in range(ends)])]
    unnamed x10 -> x32, local copies, waits for them, and re-layouts: 0.04 us -> 8.38 us
  transfers between devices with their start and end apart: 108 -> 108, of which waited for: 49 -> 50; matrix products, arithmetic and copies ran while one was open for 4% -> 4% of each run, Pallas kernels for 0% -> 0%
where the time goes in v1:
time: 697 us; the launch traced here: 685 us
  starting transfers between devices  216 us (31%)
  waiting for transfers between devices  195 us (28%)
  local copies, waits for them, and re-layouts  116 us (17%)
  blocking collectives  84.9 us (12%)
  other arithmetic  63.1 us (9%)
  between operations  9.8 us (1%)
    ppermute x54, waiting for transfers between devices, padded_2(): lax.ppermute(tail, axis, [(i, (i + 1) % count) for i in range(ends)])  195 us
    ppermute x54, starting transfers between devices, padded_2(): lax.ppermute(head, axis, [((i + 1) % count, i) for i in range(ends)])  116 us
    ppermute x54, starting transfers between devices, padded_2(): lax.ppermute(tail, axis, [(i, (i + 1) % count) for i in range(ends)])  99.7 us
    reshape x12, local copies, waits for them, and re-layouts, restrict(): blocks = values.reshape(rows // 2, 2, columns // 2, 2)  55.2 us
    all_gather x4, blocking collectives, gather_early(): return lax.all_gather(row_band, 'gx', axis=0, tiled=True)  52.7 us
    mul x13, other arithmetic, restrict(): 0.25 * (blocks[:, 0, :, 0] + blocks[:, 1, :, 0] + blocks[:, 0, :, 1] + bl...  48.1 us
    all_gather x4, blocking collectives, gather_early(): pieces = lax.all_gather(field, 'gy')  32.2 us
    reshape x10, local copies, waits for them, and re-layouts, prolong(): return copies.reshape(2 * rows, 2 * columns)  27.8 us
  transfers between devices with their start and end apart: 108, of which 50 were waited for; matrix products, arithmetic and copies ran while one was open for 4% of the time, Pallas kernels for 0%

profile of v1, /device:TPU:28, one launch (start us, length us, event | category | flops | bytes accessed | tf_op | source)
XLA Modules:
  0.0 684.8 jit_solution(17025281811054120344)
XLA Ops:
  5.3 10.5 %reshape.369 = f32[64,2,128,2]{3,2,1,0:T(8,128)} reshape(f32[128,256]{1,0:T(8,128)} %param.3) | data formatting | bytes 262144 | tf_op jit(solution)/shard_map/reshape | solution.py:30
  20.4 8.0 %fusion.1 = f32[64,128]{1,0:T(8,128)S(1)} fusion(f32[64,2,128,2]{3,2,1,0:T(8,128)} %reshape.369), kind=kLoop, calls=%fused_computation.2 | loop fusion | flops 32768 | bytes 163840 | tf_op jit(solution)/shard_map/mul | solution.py:31
  30.7 4.5 collective-permute-start.4
  50.5 9.8 %reshape.368 = f32[64,2,128,2]{3,2,1,0:T(8,128)} reshape(f32[128,256]{1,0:T(8,128)S(1)} %fusion.35) | data formatting | bytes 262144 | tf_op jit(solution)/shard_map/reshape | solution.py:30
  60.3 8.5 %multiply_reduce_fusion = (f32[64,128]{1,0:T(8,128)S(1)}, f32[64,128]{1,0:T(8,128)S(1)}) fusion(f32[64,2,128,2]{3,2,1,0:T(8,128)} %reshape.368), kind=kLoop, calls=%fused_computation.8 | loop fusion | flops 40960 | bytes 196608 | tf_op jit(solution)/shard_map/mul | solution.py:31
  81.4 8.8 %all-gather.1 = f32[128,1,32,1]{2,3,1,0:T(1,128)S(1)} all-gather(f32[16,1,32,1]{2,3,1,0:T(1,128)S(1)} %bitcast.40), channel_id=3, replica_groups=mesh['gx'=4,'gy'=8] {'gy'}, dimensions={0}, use_global_device_ids=true | all-gather | bytes 18432 | tf_op jit(solution)/shard_map/all_gather | solution.py:84
  94.4 13.3 %all_gather.31 = f32[64,256]{1,0:T(8,128)S(1)} all-gather(f32[16,256]{1,0:T(8,128)S(1)} %reshape.375), channel_id=1, replica_groups=mesh['gx'=4,'gy'=8] {'gx'}, dimensions={0}, use_global_device_ids=true | all-gather | bytes 81920 | tf_op jit(solution)/shard_map/all_gather | solution.py:86
  107.7 5.5 reshape.377
  158.9 7.8 %all-gather = f32[128,1,32,1]{2,3,1,0:T(1,128)S(1)} all-gather(f32[16,1,32,1]{2,3,1,0:T(1,128)S(1)} %bitcast.41), channel_id=2, replica_groups=mesh['gx'=4,'gy'=8] {'gy'}, dimensions={0}, use_global_device_ids=true | all-gather | bytes 18432 | tf_op jit(solution)/shard_map/all_gather | solution.py:84
  166.8 13.1 %all_gather.29 = f32[64,256]{1,0:T(8,128)S(1)} all-gather(f32[16,256]{1,0:T(8,128)S(1)} %reshape.373), channel_id=1, replica_groups=mesh['gx'=4,'gy'=8] {'gx'}, dimensions={0}, use_global_device_ids=true | all-gather | bytes 81920 | tf_op jit(solution)/shard_map/all_gather | solution.py:86
  180.2 5.6 reshape.376
  185.8 8.6 %multiply_reduce_fusion.6 = (f32[32,128]{1,0:T(8,128)S(1)}, f32[32,1,128,1]{3,2,1,0:T(8,128)S(1)}, f32[]{:T(128)}, f32[32,128]{1,0:T(8,128)S(1)}) fusion(f32[32,2,128,2]{3,2,1,0:T(8,128)} %reshape.377, f32[32,2,128,2]{3,2,1,0:T(8,128)} %reshape.376), kind=kLoop, calls=%fused_computation.33 | loop fusion | flops 36863 | bytes 180228 | tf_op jit(solution)/shard_map/mul | solution.py:31
  207.2 5.6 reshape.379
  212.8 5.8 fusion.723
  314.3 7.8 %all-gather.2 = f32[128,1,32,1]{2,3,1,0:T(1,128)S(1)} all-gather(f32[16,1,32,1]{2,3,1,0:T(1,128)S(1)} %bitcast.42), channel_id=4, replica_groups=mesh['gx'=4,'gy'=8] {'gy'}, dimensions={0}, use_global_device_ids=true | all-gather | bytes 18432 | tf_op jit(solution)/shard_map/all_gather | solution.py:84
  322.3 13.1 %all_gather.33 = f32[64,256]{1,0:T(8,128)S(1)} all-gather(f32[16,256]{1,0:T(8,128)S(1)} %reshape.384), channel_id=1, replica_groups=mesh['gx'=4,'gy'=8] {'gx'}, dimensions={0}, use_global_device_ids=true | all-gather | bytes 81920 | tf_op jit(solution)/shard_map/all_gather | solution.py:86
  335.7 5.6 reshape.385
  341.2 5.9 fusion.722
  515.9 7.8 %all-gather.3 = f32[128,1,32,1]{2,3,1,0:T(1,128)S(1)} all-gather(f32[16,1,32,1]{2,3,1,0:T(1,128)S(1)} %bitcast.43), channel_id=5, replica_groups=mesh['gx'=4,'gy'=8] {'gy'}, dimensions={0}, use_global_device_ids=true | all-gather | bytes 18432 | tf_op jit(solution)/shard_map/all_gather | solution.py:84
  523.8 13.1 %all_gather.35 = f32[64,256]{1,0:T(8,128)S(1)} all-gather(f32[16,256]{1,0:T(8,128)S(1)} %reshape.392), channel_id=1, replica_groups=mesh['gx'=4,'gy'=8] {'gx'}, dimensions={0}, use_global_device_ids=true | all-gather | bytes 81920 | tf_op jit(solution)/shard_map/all_gather | solution.py:86
  537.2 5.6 reshape.393
  542.8 5.9 fusion.721
  628.4 6.9 %reshape.397 = f32[128,256]{1,0:T(8,128)S(1)} reshape(f32[64,2,128,2]{3,2,1,0:T(8,128)} %broadcast_in_dim.29) | data formatting | bytes 262144 | tf_op jit(solution)/shard_map/reshape | solution.py:39
  638.6 4.2 collective-permute-done.97
  (478 shorter events, 483.8 us)
Async XLA Ops:
  1.6 14.2 %collective-permute-start = (f32[1,256]{1,0:T(1,128)S(1)}, f32[1,256]{1,0:T(1,128)S(1)}, u32[]{:S(2)}, u32[]{:S(2)}) collective-permute-start(f32[1,256]{1,0:T(1,128)S(1)} %get-tuple-element.53), channel_id=1, source_target_pairs={{8,0},{16,8},{24,16},{9,1},{17,9},{25,17},{10,2},{18,10},{26,18},{... | collective-permute-start | bytes 3080 | tf_op jit(solution)/shard_map/ppermute | solution.py:21
  4.0 11.8 %collective-permute-start.1 = (f32[1,256]{1,0:T(1,128)S(1)}, f32[1,256]{1,0:T(1,128)S(1)}, u32[]{:S(2)}, u32[]{:S(2)}) collective-permute-start(f32[1,256]{1,0:T(1,128)S(1)} %get-tuple-element.52), channel_id=1, source_target_pairs={{0,8},{8,16},{16,24},{1,9},{9,17},{17,25},{2,10},{10,18},{18,26},{... | collective-permute-start | bytes 3080 | tf_op jit(solution)/shard_map/ppermute | solution.py:19
  15.9 14.5 %collective-permute-start.2 = (f32[130,1]{1,0:T(8,128)S(1)}, f32[130,1]{1,0:T(8,128)S(1)}, u32[]{:S(2)}, u32[]{:S(2)}) collective-permute-start(f32[130,1]{1,0:T(8,128)S(1)} %get-tuple-element.42), channel_id=1, source_target_pairs={{1,0},{2,1},{3,2},{4,3},{5,4},{6,5},{7,6},{9,8},{10,9},{11,10},{12... | collective-permute-start | bytes 1568 | tf_op jit(solution)/shard_map/ppermute | solution.py:21
  18.5 12.0 %collective-permute-start.3 = (f32[130,1]{1,0:T(8,128)S(1)}, f32[130,1]{1,0:T(8,128)S(1)}, u32[]{:S(2)}, u32[]{:S(2)}) collective-permute-start(f32[130,1]{1,0:T(8,128)S(1)} %get-tuple-element.43), channel_id=1, source_target_pairs={{0,1},{1,2},{2,3},{3,4},{4,5},{5,6},{6,7},{8,9},{9,10},{10,11},{11... | collective-permute-start | bytes 1568 | tf_op jit(solution)/shard_map/ppermute | solution.py:19
  30.7 7.2 %collective-permute-start.4 = (f32[1,256]{1,0:T(1,128)S(1)}, f32[1,256]{1,0:T(1,128)S(1)}, u32[]{:S(2)}, u32[]{:S(2)}) collective-permute-start(f32[1,256]{1,0:T(1,128)S(1)} %get-tuple-element.51), channel_id=1, source_target_pairs={{8,0},{16,8},{24,16},{9,1},{17,9},{25,17},{10,2},{18,10},{26,18},{... | collective-permute-start | bytes 3080 | tf_op jit(solution)/shard_map/ppermute | solution.py:21
  43.8 6.5 collective-permute-start.7
  77.0 13.2 %collective-permute-start.10 = (f32[66,1]{1,0:T(8,128)S(1)}, f32[66,1]{1,0:T(8,128)S(1)}, u32[]{:S(2)}, u32[]{:S(2)}) collective-permute-start(f32[66,1]{1,0:T(8,128)S(1)} %get-tuple-element.72), channel_id=1, source_target_pairs={{1,0},{2,1},{3,2},{4,3},{5,4},{6,5},{7,6},{9,8},{10,9},{11,10},{12... | collective-permute-start | bytes 800 | tf_op jit(solution)/shard_map/ppermute | solution.py:21
  78.9 11.3 %collective-permute-start.11 = (f32[66,1]{1,0:T(8,128)S(1)}, f32[66,1]{1,0:T(8,128)S(1)}, u32[]{:S(2)}, u32[]{:S(2)}) collective-permute-start(f32[66,1]{1,0:T(8,128)S(1)} %get-tuple-element.73), channel_id=1, source_target_pairs={{0,1},{1,2},{2,3},{3,4},{4,5},{5,6},{6,7},{8,9},{9,10},{10,11},{11... | collective-permute-start | bytes 800 | tf_op jit(solution)/shard_map/ppermute | solution.py:19
  90.4 22.9 %collective-permute-start.12 = (f32[1,128]{1,0:T(1,128)S(1)}, f32[1,128]{1,0:T(1,128)S(1)}, u32[]{:S(2)}, u32[]{:S(2)}) collective-permute-start(f32[1,128]{1,0:T(1,128)S(1)} %get-tuple-element.89), channel_id=1, source_target_pairs={{8,0},{16,8},{24,16},{9,1},{17,9},{25,17},{10,2},{18,10},{26,18},{... | collective-permute-start | bytes 1544 | tf_op jit(solution)/shard_map/ppermute | solution.py:21
  92.8 20.5 %collective-permute-start.13 = (f32[1,128]{1,0:T(1,128)S(1)}, f32[1,128]{1,0:T(1,128)S(1)}, u32[]{:S(2)}, u32[]{:S(2)}) collective-permute-start(f32[1,128]{1,0:T(1,128)S(1)} %get-tuple-element.88), channel_id=1, source_target_pairs={{0,8},{8,16},{16,24},{1,9},{9,17},{17,25},{2,10},{10,18},{18,26},{... | collective-permute-start | bytes 1544 | tf_op jit(solution)/shard_map/ppermute | solution.py:19
  115.3 6.2 collective-permute-start.15
  272.1 6.0 collective-permute-start.35
  287.6 6.0 collective-permute-start.39
  303.1 6.0 collective-permute-start.43
  403.7 6.2 collective-permute-start.55
  419.4 6.2 collective-permute-start.59
  435.3 6.2 collective-permute-start.63
  451.0 6.2 collective-permute-start.67
  466.7 6.2 collective-permute-start.71
  602.4 6.2 collective-permute-start.91
  618.1 6.2 collective-permute-start.95
  644.8 6.5 collective-permute-start.99
  660.9 6.5 collective-permute-start.103
  677.0 6.5 collective-permute-start.107
  (92 other events, 529.6 us)
